TPU v7x, 256 devices: a whole 4x4x8 slice. The times are simulated.
256 devices in a mesh: panel: 2 (over core), ang: 32 (over z, x), rad: 4 (over y).
Axes of the slice: x: 4, y: 4, z: 8, core: 2. Of those that a mesh axis runs over, the one named last changes fastest.
Arguments:
- density: float32 [2, 8, 512, 512], P('panel', 'rad', 'ang'), may hold values from 1 to 2
- momentum: float32 [2, 3, 8, 512, 512], P('panel', None, 'rad', 'ang'), may hold values from -2.5 to 2.5
- magnetic: float32 [2, 3, 8, 512, 512], P('panel', None, 'rad', 'ang'), may hold values from -2.5 to 2.5
- partner_device: int32 [2, 1024, 1], P('panel', 'ang'), may hold values from 0 to 31; in each aligned block of 32 rows (0 to 31, 32 to 63, ..., all dimensions but the last counted through in order) at most 2 rows name the same one
- partner_phi: int32 [2, 1024], P('panel', 'ang'), may hold values from 0 to 14
- partner_theta: int32 [2, 1024], P('panel', 'ang'), may hold values from 0 to 510
- partner_weight: float32 [2, 1024, 4], P('panel', 'ang'), may hold values from 0 to 1, as said below
- border_turn: float32 [2, 1024], P('panel', 'ang'), may hold values from -3.140625 to 3.140625
Outputs:
- density_next: float32 [2, 8, 512, 512], P('panel', 'rad', 'ang')
- momentum_next: float32 [2, 3, 8, 512, 512], P('panel', None, 'rad', 'ang')
- magnetic_next: float32 [2, 3, 8, 512, 512], P('panel', None, 'rad', 'ang')
Inputs may be any that keep to these rules, and one draw needn't show every extreme that they name: `partner_device`: within the 32 table rows of one device (aligned blocks), at most 2 rows name the same source device. `partner_weight`: each row's weights are (1-u)(1-v), (1-u)v, u(1-v), uv for some u, v in [0, 1].
All inputs are finite; a program needn't handle non-finite values.
Results may differ from a plain program's by a relative error of at most 0.00005.
Values sent between devices are 32-bit elements; how exact they have to be, the bound alone decides.
No kernel may reach another device: no remote copies, remote signals or barrier semaphores. Data moves between devices by JAX's collectives and lax.ppermute only.
A program may use at most 64 MiB of HBM per device.

v0:
```python
import math
import jax
import jax.numpy as jnp
from jax import lax
from jax.sharding import PartitionSpec as P

time_step = 0.15
sound_sq = 1.0
viscosity = 0.1
resistivity = 0.1
r_inner = 0.35


def swapped(block, axis, apart):
    count = lax.axis_size(axis)
    route = []
    for low in range(count):
        high = low | 1 << apart
        if high != low and high < count:
            route += [(low, high), (high, low)]
    return lax.ppermute(block, axis, route)


def padded(value, sides, width):
    for axis, dim in sides:
        size, length = (lax.axis_size(axis), value.shape[dim])
        up = [(i, (i + 1) % size) for i in range(size - 1)]
        down = [(j, i) for i, j in up]
        last = lax.slice_in_dim(value, length - width, length, axis=dim)
        first = lax.slice_in_dim(value, 0, width, axis=dim)
        before = lax.ppermute(last, axis, up)
        after = lax.ppermute(first, axis, down)
        value = jnp.concatenate([before, value, after], axis=dim)
    return value


def field_of(block, index):
    return block[..., index, :, :, :]


def fluxes(block, direction):
    mass_field = field_of(block, 0)
    moment = [field_of(block, 1 + component) for component in range(3)]
    magnet = [field_of(block, 4 + component) for component in range(3)]
    velocity = [moment[component] / mass_field for component in range(3)]
    pressure = sound_sq * mass_field + 0.5 * (
        magnet[0] * magnet[0] + magnet[1] * magnet[1] + magnet[2] * magnet[2]
    )
    pieces = [moment[direction]]
    for component in range(3):
        flux_term = moment[component] * velocity[direction] - magnet[component] * magnet[direction]
        if component == direction:
            flux_term = flux_term + pressure
        pieces.append(flux_term)
    for component in range(3):
        pieces.append(
            velocity[direction] * magnet[component] - magnet[direction] * velocity[component]
        )
    return jnp.stack(pieces, axis=-4)


def tendency(current, radial, polar, azimuth, half_t, half_p, sq_t, sq_p):
    flux_r = fluxes(radial, 0)
    flux_t = fluxes(polar, 1)
    flux_p = fluxes(azimuth, 2)
    divergence = (flux_r[..., 2:, :, :] - flux_r[..., :-2, :, :]) * 0.5
    divergence = divergence + (flux_t[..., 2:] - flux_t[..., :-2]) * half_t
    divergence = divergence + (flux_p[..., :, 2:, :] - flux_p[..., :, :-2, :]) * half_p
    laplace_sum = radial[..., 2:, :, :] - 2.0 * current + radial[..., :-2, :, :]
    laplace_sum = laplace_sum + (polar[..., 2:] - 2.0 * current + polar[..., :-2]) * sq_t
    laplace_sum = (
        laplace_sum + (azimuth[..., :, 2:, :] - 2.0 * current + azimuth[..., :, :-2, :]) * sq_p
    )
    mixing = jnp.array(
        [0.0, viscosity, viscosity, viscosity, resistivity, resistivity, resistivity], jnp.float32
    ).reshape(7, 1, 1, 1)
    return mixing * laplace_sum - divergence


def turn_frame(ghost, cosine, sine):
    pieces = [ghost[0], ghost[1]]
    pieces.append(cosine * ghost[2] + sine * ghost[3])
    pieces.append(cosine * ghost[3] - sine * ghost[2])
    pieces.append(ghost[4])
    pieces.append(cosine * ghost[5] + sine * ghost[6])
    pieces.append(cosine * ghost[6] - sine * ghost[5])
    return jnp.stack(pieces, axis=0)


def route_request(packed):
    crossed = swapped(packed, "panel", 0)
    return lax.all_to_all(crossed, "ang", split_axis=0, concat_axis=0, tiled=True)


def route_reply(answer):
    crossed = swapped(answer, "panel", 0)
    return lax.all_to_all(crossed, "ang", split_axis=1, concat_axis=1, tiled=True)


def body(
    density,
    momentum,
    magnetic,
    partner_device,
    partner_phi,
    partner_theta,
    partner_weight,
    border_turn,
):
    fields_now = jnp.concatenate([density, momentum[0], magnetic[0]], axis=0)
    fields, rows_r, rows_p, rows_t = fields_now.shape
    n_ang = lax.axis_size("ang")
    n_rad = lax.axis_size("rad")
    border = partner_phi.shape[1]
    capacity = max(2, 2 * border // n_ang)
    slot_count = n_ang * capacity
    stacked_rows = fields * rows_r
    highest = lax.Precision.HIGHEST
    level = lax.axis_index("rad") * rows_r + jnp.arange(rows_r, dtype=jnp.int32)
    radius = r_inner + (level.astype(jnp.float32) + 0.5) * ((1.0 - r_inner) / (rows_r * n_rad))
    colatitude = math.pi / 4 + (jnp.arange(rows_t).astype(jnp.float32) + 0.5) * (
        math.pi / 2 / rows_t
    )
    inv_radius = (1.0 / radius).reshape(rows_r, 1, 1)
    inv_both = inv_radius / jnp.sin(colatitude)
    half_t = 0.5 * inv_radius
    half_p = 0.5 * inv_both
    sq_t = inv_radius * inv_radius
    sq_p = inv_both * inv_both
    mirror = jnp.array([1.0, -1.0, -1.0, -1.0, 1.0, 1.0, 1.0], jnp.float32).reshape(7, 1, 1, 1)
    first_r = lax.axis_index("rad") == 0
    last_r = lax.axis_index("rad") == n_rad - 1
    first_p = lax.axis_index("ang") == 0
    last_p = lax.axis_index("ang") == n_ang - 1
    source_ang = partner_device[0, :, 0]
    one_hot = (source_ang[:, None] == jnp.arange(n_ang, dtype=jnp.int32)[None, :]).astype(jnp.int32)
    ranked = jnp.sum(one_hot * (jnp.cumsum(one_hot, axis=0) - 1), axis=1)
    target_slot = source_ang * capacity + ranked
    placing = (jnp.arange(slot_count, dtype=jnp.int32)[:, None] == target_slot[None, :]).astype(
        jnp.float32
    )
    base_cell = (partner_phi[0] * rows_t + partner_theta[0]).astype(jnp.float32)
    weights = partner_weight[0]
    payload = base_cell[:, None]
    packed = jnp.dot(placing, payload, precision=highest).reshape(n_ang, capacity, payload.shape[1])
    asked = route_request(packed)
    cell_index = (asked[:, :, 0].reshape(slot_count) + 0.5).astype(jnp.int32)
    offsets = jnp.array([0, 1, rows_t, rows_t + 1], jnp.int32)
    gather_index = (cell_index[:, None] + offsets[None, :]).reshape(slot_count * 4)
    cosine = jnp.cos(border_turn[0])
    sine = jnp.sin(border_turn[0])

    def overset(current):
        table = current.reshape(stacked_rows, rows_p * rows_t)
        corner = jnp.take(table, gather_index, axis=1).reshape(stacked_rows, slot_count, 4)
        returned = route_reply(corner.reshape(stacked_rows, n_ang, capacity, 4)).reshape(
            stacked_rows, slot_count, 4
        )
        picked = [jnp.dot(returned[:, :, index], placing, precision=highest) for index in range(4)]
        ghost = weights[:, 0] * picked[0] + weights[:, 1] * picked[1]
        ghost = ghost + weights[:, 2] * picked[2]
        ghost = ghost + weights[:, 3] * picked[3]
        ghost = turn_frame(ghost.reshape(fields, rows_r, border), cosine, sine)
        return (ghost[:, :, :rows_p], ghost[:, :, rows_p:])

    def evaluate(current):
        haloed = padded(current, (("ang", 2), ("rad", 1)), 1)
        lower_r = jnp.where(first_r, mirror * current[:, :1], haloed[:, :1, 1:-1])
        upper_r = jnp.where(last_r, mirror * current[:, -1:], haloed[:, -1:, 1:-1])
        lower_p = jnp.where(first_p, mirror * current[:, :, :1], haloed[:, 1:-1, :1])
        upper_p = jnp.where(last_p, mirror * current[:, :, -1:], haloed[:, 1:-1, -1:])
        radial = jnp.concatenate([lower_r, current, upper_r], axis=1)
        azimuth = jnp.concatenate([lower_p, current, upper_p], axis=2)
        lower_t, upper_t = overset(current)
        polar = jnp.concatenate([lower_t[..., None], current, upper_t[..., None]], axis=3)
        return tendency(current, radial, polar, azimuth, half_t, half_p, sq_t, sq_p)

    slope_one = evaluate(fields_now)
    slope_two = evaluate(fields_now + 0.5 * time_step * slope_one)
    slope_three = evaluate(fields_now + 0.5 * time_step * slope_two)
    slope_four = evaluate(fields_now + time_step * slope_three)
    updated = fields_now + time_step / 6.0 * (
        slope_one + 2.0 * slope_two + 2.0 * slope_three + slope_four
    )
    return (updated[0:1], updated[1:4][None], updated[4:7][None])


def solution(mesh):
    in_specs = (
        P("panel", "rad", "ang", None),
        P("panel", None, "rad", "ang", None),
        P("panel", None, "rad", "ang", None),
        P("panel", "ang", None),
        P("panel", "ang"),
        P("panel", "ang"),
        P("panel", "ang", None),
        P("panel", "ang"),
    )
    out_specs = (
        P("panel", "rad", "ang", None),
        P("panel", None, "rad", "ang", None),
        P("panel", None, "rad", "ang", None),
    )
    return jax.shard_map(body, mesh=mesh, in_specs=in_specs, out_specs=out_specs, check_vma=False)
```

profile of v0, /device:TPU:2, one launch (start us, length us, event | category | flops | bytes accessed | tf_op | source)
XLA Modules:
  0.0 199.3 jit_solution(3785506237722466291)
XLA Ops:
  1.8 4.3 %collective-permute-start.1 = (f32[7,2,1,512]{3,2,1,0:T(1,128)S(1)}, f32[7,2,1,512]{3,2,1,0:T(1,128)S(1)}, u32[]{:S(2)}, u32[]{:S(2)}) collective-permute-start(f32[7,2,1,512]{3,2,1,0:T(1,128)S(1)} %get-tuple-element.75), channel_id=1, source_target_pairs={{4,0},{8,4},{12,8},{16,12},{20,16},{24,20},{28,24},{32,28},{36,32}... | collective-permute-start | bytes 86024 | tf_op jit(solution)/shard_map/ppermute | solution.py:32
  13.2 13.2 %all-to-all-start = ((f32[32,2,1]{1,2,0:T(1,128)}), f32[32,2,1]{1,2,0:T(1,128)S(1)}, u32[]{:S(2)}, u32[]{:S(2)}) async-start(f32[32,2,1]{1,2,0:T(1,128)} %copy.59), calls=%async_computation | async-start | bytes 32768 | tf_op jit(solution)/shard_map/all_to_all | solution.py:92
  27.5 2.7 %copy.60 = f32[14,8192]{0,1:T(8,128)} copy(f32[14,8192]{1,0:T(8,128)S(1)} %bitcast.210) | data formatting | bytes 917504 | tf_op jit(solution)/shard_map/reshape | solution.py:154
  30.2 4.7 %all-to-all-done = f32[32,2,1]{1,2,0:T(1,128)S(1)} async-done(((f32[32,2,1]{1,2,0:T(1,128)}), f32[32,2,1]{1,2,0:T(1,128)S(1)}, u32[]{:S(2)}, u32[]{:S(2)}) %all-to-all-start) | async-done | bytes 288 | tf_op jit(solution)/shard_map/all_to_all | solution.py:92
  35.3 2.9 %gather_fusion = f32[256,14]{1,0:T(8,128)S(1)} fusion(f32[14,8192]{0,1:T(8,128)} %copy.60, s32[1024]{0:T(1024)S(1)} %pad_clamp_fusion), kind=kCustom, calls=%fused_computation.clone | custom fusion | bytes 29696 | tf_op jit(solution)/shard_map/jit(_take)/gather | solution.py:155
  39.9 5.1 %all-to-all-start.1 = ((f32[14,32,2,4]{0,3,2,1:T(4,128)}), f32[14,32,2,4]{0,3,2,1:T(4,128)S(1)}, u32[]{:S(2)}, u32[]{:S(2)}) async-start(f32[14,32,2,4]{0,3,2,1:T(4,128)} %collective-permute-done.5), calls=%async_computation.1 | async-start | bytes 262144 | tf_op jit(solution)/shard_map/all_to_all | solution.py:97
  46.4 4.2 %collective-permute-start.3 = (f32[7,1,18,512]{3,2,1,0:T(8,128)}, f32[7,1,18,512]{3,2,1,0:T(8,128)}, u32[]{:S(2)}, u32[]{:S(2)}) collective-permute-start(f32[7,1,18,512]{3,2,1,0:T(8,128)} %get-tuple-element.40), channel_id=1, source_target_pairs={{0,1},{1,2},{2,3},{4,5},{5,6},{6,7},{8,9},{9,10},{10,11},{12,13},{... | collective-permute-start | bytes 774152 | tf_op jit(solution)/shard_map/ppermute | solution.py:31
  57.4 4.6 %collective-permute-done.2 = f32[7,1,18,512]{3,2,1,0:T(8,128)} collective-permute-done((f32[7,1,18,512]{3,2,1,0:T(8,128)S(1)}, f32[7,1,18,512]{3,2,1,0:T(8,128)}, u32[]{:S(2)}, u32[]{:S(2)}) %collective-permute-start.2) | collective-permute-done | bytes 258080 | tf_op jit(solution)/shard_map/ppermute | solution.py:32
  67.0 3.3 %collective-permute-start.6 = (f32[7,2,1,512]{3,2,1,0:T(1,128)S(1)}, f32[7,2,1,512]{3,2,1,0:T(1,128)S(1)}, u32[]{:S(2)}, u32[]{:S(2)}) collective-permute-start(f32[7,2,1,512]{3,2,1,0:T(1,128)S(1)} %get-tuple-element.70), channel_id=1, source_target_pairs={{0,4},{4,8},{8,12},{12,16},{16,20},{20,24},{24,28},{28,32},{32,36}... | collective-permute-start | bytes 86024 | tf_op jit(solution)/shard_map/ppermute | solution.py:31
  73.3 2.9 %gather_fusion.1 = f32[256,14]{1,0:T(8,128)S(1)} fusion(f32[14,8192]{0,1:T(8,128)} %copy.65, s32[1024]{0:T(1024)S(1)} %pad_clamp_fusion), kind=kCustom, calls=%fused_computation.1.clone | custom fusion | bytes 29696 | tf_op jit(solution)/shard_map/jit(_take)/gather | solution.py:155
  77.9 11.7 %all-to-all-start.2 = ((f32[14,32,2,4]{0,3,2,1:T(4,128)}), f32[14,32,2,4]{0,3,2,1:T(4,128)S(1)}, u32[]{:S(2)}, u32[]{:S(2)}) async-start(f32[14,32,2,4]{0,3,2,1:T(4,128)} %collective-permute-done.10), calls=%async_computation.2 | async-start | bytes 262144 | tf_op jit(solution)/shard_map/all_to_all | solution.py:97
  91.2 3.5 %collective-permute-start.9 = (f32[7,1,18,512]{3,2,1,0:T(8,128)}, f32[7,1,18,512]{3,2,1,0:T(8,128)}, u32[]{:S(2)}, u32[]{:S(2)}) collective-permute-start(f32[7,1,18,512]{3,2,1,0:T(8,128)} %get-tuple-element.38), channel_id=1, source_target_pairs={{0,1},{1,2},{2,3},{4,5},{5,6},{6,7},{8,9},{9,10},{10,11},{12,13},{... | collective-permute-start | bytes 774152 | tf_op jit(solution)/shard_map/ppermute | solution.py:31
  96.0 2.8 %all-to-all-done.2 = f32[14,32,2,4]{0,3,2,1:T(4,128)S(1)} async-done(((f32[14,32,2,4]{0,3,2,1:T(4,128)}), f32[14,32,2,4]{0,3,2,1:T(4,128)S(1)}, u32[]{:S(2)}, u32[]{:S(2)}) %all-to-all-start.2) | async-done | bytes 14368 | tf_op jit(solution)/shard_map/all_to_all | solution.py:97
  101.3 4.8 %collective-permute-done.8 = f32[7,1,18,512]{3,2,1,0:T(8,128)} collective-permute-done((f32[7,1,18,512]{3,2,1,0:T(8,128)}, f32[7,1,18,512]{3,2,1,0:T(8,128)}, u32[]{:S(2)}, u32[]{:S(2)}) %collective-permute-start.8) | collective-permute-done | bytes 258080 | tf_op jit(solution)/shard_map/ppermute | solution.py:32
  112.3 3.6 %collective-permute-start.11 = (f32[7,2,1,512]{3,2,1,0:T(1,128)S(1)}, f32[7,2,1,512]{3,2,1,0:T(1,128)S(1)}, u32[]{:S(2)}, u32[]{:S(2)}) collective-permute-start(f32[7,2,1,512]{3,2,1,0:T(1,128)S(1)} %get-tuple-element.66), channel_id=1, source_target_pairs={{0,4},{4,8},{8,12},{12,16},{16,20},{20,24},{24,28},{28,32},{32,36}... | collective-permute-start | bytes 86024 | tf_op jit(solution)/shard_map/ppermute | solution.py:31
  119.0 2.9 %gather_fusion.2 = f32[256,14]{1,0:T(8,128)S(1)} fusion(f32[14,8192]{0,1:T(8,128)} %copy.70, s32[1024]{0:T(1024)S(1)} %pad_clamp_fusion), kind=kCustom, calls=%fused_computation.2.clone | custom fusion | bytes 29696 | tf_op jit(solution)/shard_map/jit(_take)/gather | solution.py:155
  123.5 11.6 %all-to-all-start.3 = ((f32[14,32,2,4]{0,3,2,1:T(4,128)}), f32[14,32,2,4]{0,3,2,1:T(4,128)S(1)}, u32[]{:S(2)}, u32[]{:S(2)}) async-start(f32[14,32,2,4]{0,3,2,1:T(4,128)} %collective-permute-done.15), calls=%async_computation.3 | async-start | bytes 262144 | tf_op jit(solution)/shard_map/all_to_all | solution.py:97
  137.5 3.2 %collective-permute-start.14 = (f32[7,1,18,512]{3,2,1,0:T(8,128)}, f32[7,1,18,512]{3,2,1,0:T(8,128)}, u32[]{:S(2)}, u32[]{:S(2)}) collective-permute-start(f32[7,1,18,512]{3,2,1,0:T(8,128)} %get-tuple-element.36), channel_id=1, source_target_pairs={{0,1},{1,2},{2,3},{4,5},{5,6},{6,7},{8,9},{9,10},{10,11},{12,13},{... | collective-permute-start | bytes 774152 | tf_op jit(solution)/shard_map/ppermute | solution.py:31
  147.3 4.6 %collective-permute-done.13 = f32[7,1,18,512]{3,2,1,0:T(8,128)} collective-permute-done((f32[7,1,18,512]{3,2,1,0:T(8,128)S(1)}, f32[7,1,18,512]{3,2,1,0:T(8,128)}, u32[]{:S(2)}, u32[]{:S(2)}) %collective-permute-start.13) | collective-permute-done | bytes 258080 | tf_op jit(solution)/shard_map/ppermute | solution.py:32
  156.7 3.4 %collective-permute-start.16 = (f32[7,2,1,512]{3,2,1,0:T(1,128)S(1)}, f32[7,2,1,512]{3,2,1,0:T(1,128)S(1)}, u32[]{:S(2)}, u32[]{:S(2)}) collective-permute-start(f32[7,2,1,512]{3,2,1,0:T(1,128)S(1)} %get-tuple-element.62), channel_id=1, source_target_pairs={{0,4},{4,8},{8,12},{12,16},{16,20},{20,24},{24,28},{28,32},{32,36}... | collective-permute-start | bytes 86024 | tf_op jit(solution)/shard_map/ppermute | solution.py:31
  163.2 2.9 %gather_fusion.3 = f32[256,14]{1,0:T(8,128)S(1)} fusion(f32[14,8192]{0,1:T(8,128)} %copy.75, s32[1024]{0:T(1024)S(1)} %pad_clamp_fusion), kind=kCustom, calls=%fused_computation.3.clone | custom fusion | bytes 29696 | tf_op jit(solution)/shard_map/jit(_take)/gather | solution.py:155
  167.8 11.6 %all-to-all-start.4 = ((f32[14,32,2,4]{0,3,2,1:T(4,128)}), f32[14,32,2,4]{0,3,2,1:T(4,128)S(1)}, u32[]{:S(2)}, u32[]{:S(2)}) async-start(f32[14,32,2,4]{0,3,2,1:T(4,128)} %collective-permute-done.20), calls=%async_computation.4 | async-start | bytes 262144 | tf_op jit(solution)/shard_map/all_to_all | solution.py:97
  185.2 3.2 %all-to-all-done.4 = f32[14,32,2,4]{0,3,2,1:T(4,128)S(1)} async-done(((f32[14,32,2,4]{0,3,2,1:T(4,128)}), f32[14,32,2,4]{0,3,2,1:T(4,128)S(1)}, u32[]{:S(2)}, u32[]{:S(2)}) %all-to-all-start.4) | async-done | bytes 14368 | tf_op jit(solution)/shard_map/all_to_all | solution.py:97
  190.7 4.6 %collective-permute-done.18 = f32[7,1,18,512]{3,2,1,0:T(8,128)} collective-permute-done((f32[7,1,18,512]{3,2,1,0:T(8,128)S(1)}, f32[7,1,18,512]{3,2,1,0:T(8,128)}, u32[]{:S(2)}, u32[]{:S(2)}) %collective-permute-start.18) | collective-permute-done | bytes 258080 | tf_op jit(solution)/shard_map/ppermute | solution.py:32
  (270 shorter events, 74.9 us)
Async XLA Ops:
  1.8 43.1 %collective-permute-start.1 = (f32[7,2,1,512]{3,2,1,0:T(1,128)S(1)}, f32[7,2,1,512]{3,2,1,0:T(1,128)S(1)}, u32[]{:S(2)}, u32[]{:S(2)}) collective-permute-start(f32[7,2,1,512]{3,2,1,0:T(1,128)S(1)} %get-tuple-element.75), channel_id=1, source_target_pairs={{4,0},{8,4},{12,8},{16,12},{20,16},{24,20},{28,24},{32,28},{36,32}... | collective-permute-start | bytes 86024 | tf_op jit(solution)/shard_map/ppermute | solution.py:32
  6.1 38.8 %collective-permute-start = (f32[7,2,1,512]{3,2,1,0:T(1,128)S(1)}, f32[7,2,1,512]{3,2,1,0:T(1,128)S(1)}, u32[]{:S(2)}, u32[]{:S(2)}) collective-permute-start(f32[7,2,1,512]{3,2,1,0:T(1,128)S(1)} %get-tuple-element.74), channel_id=1, source_target_pairs={{0,4},{4,8},{8,12},{12,16},{16,20},{20,24},{24,28},{28,32},{32,36}... | collective-permute-start | bytes 86024 | tf_op jit(solution)/shard_map/ppermute | solution.py:31
  13.2 21.7 %all-to-all-start = ((f32[32,2,1]{1,2,0:T(1,128)}), f32[32,2,1]{1,2,0:T(1,128)S(1)}, u32[]{:S(2)}, u32[]{:S(2)}) async-start(f32[32,2,1]{1,2,0:T(1,128)} %copy.59), calls=%async_computation | async-start | bytes 32768 | tf_op jit(solution)/shard_map/all_to_all | solution.py:92
  38.3 1.6 collective-permute-start.5
  39.9 14.2 %all-to-all-start.1 = ((f32[14,32,2,4]{0,3,2,1:T(4,128)}), f32[14,32,2,4]{0,3,2,1:T(4,128)S(1)}, u32[]{:S(2)}, u32[]{:S(2)}) async-start(f32[14,32,2,4]{0,3,2,1:T(4,128)} %collective-permute-done.5), calls=%async_computation.1 | async-start | bytes 262144 | tf_op jit(solution)/shard_map/all_to_all | solution.py:97
  46.4 11.0 %collective-permute-start.3 = (f32[7,1,18,512]{3,2,1,0:T(8,128)}, f32[7,1,18,512]{3,2,1,0:T(8,128)}, u32[]{:S(2)}, u32[]{:S(2)}) collective-permute-start(f32[7,1,18,512]{3,2,1,0:T(8,128)} %get-tuple-element.40), channel_id=1, source_target_pairs={{0,1},{1,2},{2,3},{4,5},{5,6},{6,7},{8,9},{9,10},{10,11},{12,13},{... | collective-permute-start | bytes 774152 | tf_op jit(solution)/shard_map/ppermute | solution.py:31
  50.6 11.4 %collective-permute-start.2 = (f32[7,1,18,512]{3,2,1,0:T(8,128)S(1)}, f32[7,1,18,512]{3,2,1,0:T(8,128)}, u32[]{:S(2)}, u32[]{:S(2)}) collective-permute-start(f32[7,1,18,512]{3,2,1,0:T(8,128)S(1)} %get-tuple-element.41), channel_id=1, source_target_pairs={{1,0},{2,1},{3,2},{5,4},{6,5},{7,6},{9,8},{10,9},{11,10},{13,12},{... | collective-permute-start | bytes 774152 | tf_op jit(solution)/shard_map/ppermute | solution.py:32
  64.4 25.2 %collective-permute-start.7 = (f32[7,2,1,512]{3,2,1,0:T(1,128)S(1)}, f32[7,2,1,512]{3,2,1,0:T(1,128)S(1)}, u32[]{:S(2)}, u32[]{:S(2)}) collective-permute-start(f32[7,2,1,512]{3,2,1,0:T(1,128)S(1)} %get-tuple-element.71), channel_id=1, source_target_pairs={{4,0},{8,4},{12,8},{16,12},{20,16},{24,20},{28,24},{32,28},{36,32}... | collective-permute-start | bytes 86024 | tf_op jit(solution)/shard_map/ppermute | solution.py:32
  67.0 22.7 %collective-permute-start.6 = (f32[7,2,1,512]{3,2,1,0:T(1,128)S(1)}, f32[7,2,1,512]{3,2,1,0:T(1,128)S(1)}, u32[]{:S(2)}, u32[]{:S(2)}) collective-permute-start(f32[7,2,1,512]{3,2,1,0:T(1,128)S(1)} %get-tuple-element.70), channel_id=1, source_target_pairs={{0,4},{4,8},{8,12},{12,16},{16,20},{20,24},{24,28},{28,32},{32,36}... | collective-permute-start | bytes 86024 | tf_op jit(solution)/shard_map/ppermute | solution.py:31
  76.4 1.6 collective-permute-start.10
  77.9 20.8 %all-to-all-start.2 = ((f32[14,32,2,4]{0,3,2,1:T(4,128)}), f32[14,32,2,4]{0,3,2,1:T(4,128)S(1)}, u32[]{:S(2)}, u32[]{:S(2)}) async-start(f32[14,32,2,4]{0,3,2,1:T(4,128)} %collective-permute-done.10), calls=%async_computation.2 | async-start | bytes 262144 | tf_op jit(solution)/shard_map/all_to_all | solution.py:97
  91.2 10.1 %collective-permute-start.9 = (f32[7,1,18,512]{3,2,1,0:T(8,128)}, f32[7,1,18,512]{3,2,1,0:T(8,128)}, u32[]{:S(2)}, u32[]{:S(2)}) collective-permute-start(f32[7,1,18,512]{3,2,1,0:T(8,128)} %get-tuple-element.38), channel_id=1, source_target_pairs={{0,1},{1,2},{2,3},{4,5},{5,6},{6,7},{8,9},{9,10},{10,11},{12,13},{... | collective-permute-start | bytes 774152 | tf_op jit(solution)/shard_map/ppermute | solution.py:31
  94.7 11.5 %collective-permute-start.8 = (f32[7,1,18,512]{3,2,1,0:T(8,128)}, f32[7,1,18,512]{3,2,1,0:T(8,128)}, u32[]{:S(2)}, u32[]{:S(2)}) collective-permute-start(f32[7,1,18,512]{3,2,1,0:T(8,128)} %get-tuple-element.39), channel_id=1, source_target_pairs={{1,0},{2,1},{3,2},{5,4},{6,5},{7,6},{9,8},{10,9},{11,10},{13,12},{... | collective-permute-start | bytes 774152 | tf_op jit(solution)/shard_map/ppermute | solution.py:32
  109.9 25.3 %collective-permute-start.12 = (f32[7,2,1,512]{3,2,1,0:T(1,128)S(1)}, f32[7,2,1,512]{3,2,1,0:T(1,128)S(1)}, u32[]{:S(2)}, u32[]{:S(2)}) collective-permute-start(f32[7,2,1,512]{3,2,1,0:T(1,128)S(1)} %get-tuple-element.67), channel_id=1, source_target_pairs={{4,0},{8,4},{12,8},{16,12},{20,16},{24,20},{28,24},{32,28},{36,32}... | collective-permute-start | bytes 86024 | tf_op jit(solution)/shard_map/ppermute | solution.py:32
  112.3 22.9 %collective-permute-start.11 = (f32[7,2,1,512]{3,2,1,0:T(1,128)S(1)}, f32[7,2,1,512]{3,2,1,0:T(1,128)S(1)}, u32[]{:S(2)}, u32[]{:S(2)}) collective-permute-start(f32[7,2,1,512]{3,2,1,0:T(1,128)S(1)} %get-tuple-element.66), channel_id=1, source_target_pairs={{0,4},{4,8},{8,12},{12,16},{16,20},{20,24},{24,28},{28,32},{32,36}... | collective-permute-start | bytes 86024 | tf_op jit(solution)/shard_map/ppermute | solution.py:31
  122.0 1.6 collective-permute-start.15
  123.5 20.7 %all-to-all-start.3 = ((f32[14,32,2,4]{0,3,2,1:T(4,128)}), f32[14,32,2,4]{0,3,2,1:T(4,128)S(1)}, u32[]{:S(2)}, u32[]{:S(2)}) async-start(f32[14,32,2,4]{0,3,2,1:T(4,128)} %collective-permute-done.15), calls=%async_computation.3 | async-start | bytes 262144 | tf_op jit(solution)/shard_map/all_to_all | solution.py:97
  137.5 9.8 %collective-permute-start.14 = (f32[7,1,18,512]{3,2,1,0:T(8,128)}, f32[7,1,18,512]{3,2,1,0:T(8,128)}, u32[]{:S(2)}, u32[]{:S(2)}) collective-permute-start(f32[7,1,18,512]{3,2,1,0:T(8,128)} %get-tuple-element.36), channel_id=1, source_target_pairs={{0,1},{1,2},{2,3},{4,5},{5,6},{6,7},{8,9},{9,10},{10,11},{12,13},{... | collective-permute-start | bytes 774152 | tf_op jit(solution)/shard_map/ppermute | solution.py:31
  140.7 11.3 %collective-permute-start.13 = (f32[7,1,18,512]{3,2,1,0:T(8,128)S(1)}, f32[7,1,18,512]{3,2,1,0:T(8,128)}, u32[]{:S(2)}, u32[]{:S(2)}) collective-permute-start(f32[7,1,18,512]{3,2,1,0:T(8,128)S(1)} %get-tuple-element.37), channel_id=1, source_target_pairs={{1,0},{2,1},{3,2},{5,4},{6,5},{7,6},{9,8},{10,9},{11,10},{13,12},{... | collective-permute-start | bytes 774152 | tf_op jit(solution)/shard_map/ppermute | solution.py:32
  154.3 25.1 %collective-permute-start.17 = (f32[7,2,1,512]{3,2,1,0:T(1,128)S(1)}, f32[7,2,1,512]{3,2,1,0:T(1,128)S(1)}, u32[]{:S(2)}, u32[]{:S(2)}) collective-permute-start(f32[7,2,1,512]{3,2,1,0:T(1,128)S(1)} %get-tuple-element.63), channel_id=1, source_target_pairs={{4,0},{8,4},{12,8},{16,12},{20,16},{24,20},{28,24},{32,28},{36,32}... | collective-permute-start | bytes 86024 | tf_op jit(solution)/shard_map/ppermute | solution.py:32
  156.7 22.7 %collective-permute-start.16 = (f32[7,2,1,512]{3,2,1,0:T(1,128)S(1)}, f32[7,2,1,512]{3,2,1,0:T(1,128)S(1)}, u32[]{:S(2)}, u32[]{:S(2)}) collective-permute-start(f32[7,2,1,512]{3,2,1,0:T(1,128)S(1)} %get-tuple-element.62), channel_id=1, source_target_pairs={{0,4},{4,8},{8,12},{12,16},{16,20},{20,24},{24,28},{28,32},{32,36}... | collective-permute-start | bytes 86024 | tf_op jit(solution)/shard_map/ppermute | solution.py:31
  167.8 20.7 %all-to-all-start.4 = ((f32[14,32,2,4]{0,3,2,1:T(4,128)}), f32[14,32,2,4]{0,3,2,1:T(4,128)S(1)}, u32[]{:S(2)}, u32[]{:S(2)}) async-start(f32[14,32,2,4]{0,3,2,1:T(4,128)} %collective-permute-done.20), calls=%async_computation.4 | async-start | bytes 262144 | tf_op jit(solution)/shard_map/all_to_all | solution.py:97
  181.7 8.9 %collective-permute-start.19 = (f32[7,1,18,512]{3,2,1,0:T(8,128)}, f32[7,1,18,512]{3,2,1,0:T(8,128)}, u32[]{:S(2)}, u32[]{:S(2)}) collective-permute-start(f32[7,1,18,512]{3,2,1,0:T(8,128)} %get-tuple-element.34), channel_id=1, source_target_pairs={{0,1},{1,2},{2,3},{4,5},{5,6},{6,7},{8,9},{9,10},{10,11},{12,13},{... | collective-permute-start | bytes 774152 | tf_op jit(solution)/shard_map/ppermute | solution.py:31
  183.9 11.4 %collective-permute-start.18 = (f32[7,1,18,512]{3,2,1,0:T(8,128)S(1)}, f32[7,1,18,512]{3,2,1,0:T(8,128)}, u32[]{:S(2)}, u32[]{:S(2)}) collective-permute-start(f32[7,1,18,512]{3,2,1,0:T(8,128)S(1)} %get-tuple-element.35), channel_id=1, source_target_pairs={{1,0},{2,1},{3,2},{5,4},{6,5},{7,6},{9,8},{10,9},{11,10},{13,12},{... | collective-permute-start | bytes 774152 | tf_op jit(solution)/shard_map/ppermute | solution.py:32
  (13 other events, 251.6 us)
where the time goes:
time: 200 us; the launch traced here: 199 us
  starting transfers between devices  95.8 us (48%)
  waiting for transfers between devices  43.7 us (22%)
  local copies, waits for them, and re-layouts  35.1 us (18%)
  other arithmetic  18.7 us (9%)
  matrix products  4.04 us (2%)
    all_to_all x4, starting transfers between devices, route_reply(): lax.all_to_all(crossed, 'ang', split_axis=1, concat_axis=1, tiled=True)  40 us
    ppermute x8, starting transfers between devices, padded(): before = lax.ppermute(last, axis, up)  25.4 us
    ppermute x8, waiting for transfers between devices, padded(): after = lax.ppermute(first, axis, down)  18.7 us
    ppermute x8, starting transfers between devices, padded(): after = lax.ppermute(first, axis, down)  16.8 us
    all_to_all x1, starting transfers between devices, route_request(): lax.all_to_all(crossed, 'ang', split_axis=0, concat_axis=0, tiled=True)  13.2 us
    gather x4, local copies, waits for them, and re-layouts, overset(): jnp.take(table, gather_index, axis=1).reshape(stacked_rows, slot_count, 4)  11.6 us
    reshape x4, local copies, waits for them, and re-layouts, overset(): table = current.reshape(stacked_rows, rows_p * rows_t)  10.7 us
    all_to_all x4, waiting for transfers between devices, route_reply(): lax.all_to_all(crossed, 'ang', split_axis=1, concat_axis=1, tiled=True)  10.4 us
  transfers between devices with their start and end apart: 26, of which 18 were waited for; matrix products, arithmetic and copies ran while one was open for 21% of the time, Pallas kernels for 0%

commit v1 on v0

--- a/solution.py
+++ b/solution.py
@@ -9,6 +9,12 @@
 viscosity = 0.1
 resistivity = 0.1
 r_inner = 0.35
+
+
+def supply_pieces_all(inner_x):
+    return jnp.concatenate(
+        lax.all_to_all(jnp.stack(jnp.split(inner_x, lax.axis_size("ang"), 1)), "ang", 0, 0), 1
+    )
 
 
 def swapped(block, axis, apart):
@@ -94,7 +100,7 @@
 
 def route_reply(answer):
     crossed = swapped(answer, "panel", 0)
-    return lax.all_to_all(crossed, "ang", split_axis=1, concat_axis=1, tiled=True)
+    return supply_pieces_all(crossed)
 
 
 def body(

time: 200 us -> 271 us (1.35)
  local copies, waits for them, and re-layouts: 35.1 us -> 111 us
  waiting for transfers between devices: 43.7 us -> 38.4 us
    unnamed x54 -> x178, local copies, waits for them, and re-layouts: 3.45 us -> 77 us
    ppermute x5, waiting for transfers between devices: 6.01 us -> 1.49 us  [swapped(): return lax.ppermute(block, axis, route)]
  transfers between devices with their start and end apart: 26 -> 26, of which waited for: 18 -> 15; matrix products, arithmetic and copies ran while one was open for 21% -> 37% of each run, Pallas kernels for 0% -> 0%
where the time goes in v1:
time: 271 us; the launch traced here: 270 us
  local copies, waits for them, and re-layouts  111 us (41%)
  starting transfers between devices  95.8 us (35%)
  waiting for transfers between devices  38.4 us (14%)
  other arithmetic  18.7 us (7%)
  matrix products  4.04 us (1%)
    unnamed x178, local copies, waits for them, and re-layouts  77 us
    all_to_all x4, starting transfers between devices, supply_pieces_all(): lax.all_to_all(jnp.stack(jnp.split(inner_x, lax.axis_size('ang'), 1)), 'a...  39.9 us
    ppermute x8, starting transfers between devices, padded(): before = lax.ppermute(last, axis, up)  25.2 us
    ppermute x8, waiting for transfers between devices, padded(): after = lax.ppermute(first, axis, down)  18.7 us
    ppermute x8, starting transfers between devices, padded(): after = lax.ppermute(first, axis, down)  17 us
    all_to_all x1, starting transfers between devices, route_request(): lax.all_to_all(crossed, 'ang', split_axis=0, concat_axis=0, tiled=True)  13.2 us
    gather x4, local copies, waits for them, and re-layouts, overset(): jnp.take(table, gather_index, axis=1).reshape(stacked_rows, slot_count, 4)  11.6 us
    reshape x4, local copies, waits for them, and re-layouts, overset(): table = current.reshape(stacked_rows, rows_p * rows_t)  10.7 us
  transfers between devices with their start and end apart: 26, of which 15 were waited for; matrix products, arithmetic and copies ran while one was open for 37% of the time, Pallas kernels for 0%

profile of v1, /device:TPU:2, one launch (start us, length us, event | category | flops | bytes accessed | tf_op | source)
XLA Modules:
  0.0 269.9 jit_solution(6122855452903727916)
XLA Ops:
  1.8 4.3 %collective-permute-start.1 = (f32[7,2,1,512]{3,2,1,0:T(1,128)S(1)}, f32[7,2,1,512]{3,2,1,0:T(1,128)S(1)}, u32[]{:S(2)}, u32[]{:S(2)}) collective-permute-start(f32[7,2,1,512]{3,2,1,0:T(1,128)S(1)} %get-tuple-element.75), channel_id=1, source_target_pairs={{4,0},{8,4},{12,8},{16,12},{20,16},{24,20},{28,24},{32,28},{36,32}... | collective-permute-start | bytes 86024 | tf_op jit(solution)/shard_map/ppermute | solution.py:38
  13.2 13.2 %all-to-all-start = ((f32[32,2,1]{1,2,0:T(1,128)}), f32[32,2,1]{1,2,0:T(1,128)S(1)}, u32[]{:S(2)}, u32[]{:S(2)}) async-start(f32[32,2,1]{1,2,0:T(1,128)} %copy.723), calls=%async_computation | async-start | bytes 32768 | tf_op jit(solution)/shard_map/all_to_all | solution.py:98
  30.2 4.7 %all-to-all-done = f32[32,2,1]{1,2,0:T(1,128)S(1)} async-done(((f32[32,2,1]{1,2,0:T(1,128)}), f32[32,2,1]{1,2,0:T(1,128)S(1)}, u32[]{:S(2)}, u32[]{:S(2)}) %all-to-all-start) | async-done | bytes 288 | tf_op jit(solution)/shard_map/all_to_all | solution.py:98
  35.3 2.9 %gather_fusion = f32[256,14]{1,0:T(8,128)S(1)} fusion(f32[14,8192]{0,1:T(8,128)} %copy.724, s32[1024]{0:T(1024)S(1)} %pad_clamp_fusion), kind=kCustom, calls=%fused_computation.clone | custom fusion | bytes 29696 | tf_op jit(solution)/shard_map/jit(_take)/gather | solution.py:161
  58.7 5.1 %all-to-all-start.1 = ((f32[32,14,1,2,4]{1,4,3,2,0:T(4,128)}), f32[32,14,1,2,4]{1,4,3,2,0:T(4,128)S(1)}, u32[]{:S(2)}, u32[]{:S(2)}) async-start(f32[32,14,1,2,4]{1,4,3,2,0:T(4,128)} %constant_dynamic-update-slice_fusion), calls=%async_computation.1 | async-start | bytes 262144 | tf_op jit(solution)/shard_map/all_to_all | solution.py:16
  65.3 4.2 %collective-permute-start.3 = (f32[7,1,18,512]{3,2,1,0:T(8,128)}, f32[7,1,18,512]{3,2,1,0:T(8,128)}, u32[]{:S(2)}, u32[]{:S(2)}) collective-permute-start(f32[7,1,18,512]{3,2,1,0:T(8,128)} %get-tuple-element.40), channel_id=1, source_target_pairs={{0,1},{1,2},{2,3},{4,5},{5,6},{6,7},{8,9},{9,10},{10,11},{12,13},{... | collective-permute-start | bytes 774152 | tf_op jit(solution)/shard_map/ppermute | solution.py:37
  76.3 4.6 %collective-permute-done.2 = f32[7,1,18,512]{3,2,1,0:T(8,128)} collective-permute-done((f32[7,1,18,512]{3,2,1,0:T(8,128)S(1)}, f32[7,1,18,512]{3,2,1,0:T(8,128)}, u32[]{:S(2)}, u32[]{:S(2)}) %collective-permute-start.2) | collective-permute-done | bytes 258080 | tf_op jit(solution)/shard_map/ppermute | solution.py:38
  86.3 2.9 %gather_fusion.1 = f32[256,14]{1,0:T(8,128)S(1)} fusion(f32[14,8192]{0,1:T(8,128)} %copy.734, s32[1024]{0:T(1024)S(1)} %pad_clamp_fusion), kind=kCustom, calls=%fused_computation.1.clone | custom fusion | bytes 29696 | tf_op jit(solution)/shard_map/jit(_take)/gather | solution.py:161
  92.0 3.3 %collective-permute-start.6 = (f32[7,2,1,512]{3,2,1,0:T(1,128)S(1)}, f32[7,2,1,512]{3,2,1,0:T(1,128)S(1)}, u32[]{:S(2)}, u32[]{:S(2)}) collective-permute-start(f32[7,2,1,512]{3,2,1,0:T(1,128)S(1)} %get-tuple-element.70), channel_id=1, source_target_pairs={{0,4},{4,8},{8,12},{12,16},{16,20},{20,24},{24,28},{28,32},{32,36}... | collective-permute-start | bytes 86024 | tf_op jit(solution)/shard_map/ppermute | solution.py:37
  114.3 11.7 %all-to-all-start.2 = ((f32[32,14,1,2,4]{1,4,3,2,0:T(4,128)}), f32[32,14,1,2,4]{1,4,3,2,0:T(4,128)S(1)}, u32[]{:S(2)}, u32[]{:S(2)}) async-start(f32[32,14,1,2,4]{1,4,3,2,0:T(4,128)} %constant_dynamic-update-slice_fusion.60), calls=%async_computation.2 | async-start | bytes 262144 | tf_op jit(solution)/shard_map/all_to_all | solution.py:16
  127.6 3.5 %collective-permute-start.9 = (f32[7,1,18,512]{3,2,1,0:T(8,128)}, f32[7,1,18,512]{3,2,1,0:T(8,128)}, u32[]{:S(2)}, u32[]{:S(2)}) collective-permute-start(f32[7,1,18,512]{3,2,1,0:T(8,128)} %get-tuple-element.38), channel_id=1, source_target_pairs={{0,1},{1,2},{2,3},{4,5},{5,6},{6,7},{8,9},{9,10},{10,11},{12,13},{... | collective-permute-start | bytes 774152 | tf_op jit(solution)/shard_map/ppermute | solution.py:37
  137.5 4.8 %collective-permute-done.8 = f32[7,1,18,512]{3,2,1,0:T(8,128)} collective-permute-done((f32[7,1,18,512]{3,2,1,0:T(8,128)}, f32[7,1,18,512]{3,2,1,0:T(8,128)}, u32[]{:S(2)}, u32[]{:S(2)}) %collective-permute-start.8) | collective-permute-done | bytes 258080 | tf_op jit(solution)/shard_map/ppermute | solution.py:38
  146.4 2.7 copy.744
  149.1 2.9 %gather_fusion.2 = f32[256,14]{1,0:T(8,128)S(1)} fusion(f32[14,8192]{0,1:T(8,128)} %copy.744, s32[1024]{0:T(1024)S(1)} %pad_clamp_fusion), kind=kCustom, calls=%fused_computation.2.clone | custom fusion | bytes 29696 | tf_op jit(solution)/shard_map/jit(_take)/gather | solution.py:161
  154.7 3.4 %collective-permute-start.11 = (f32[7,2,1,512]{3,2,1,0:T(1,128)S(1)}, f32[7,2,1,512]{3,2,1,0:T(1,128)S(1)}, u32[]{:S(2)}, u32[]{:S(2)}) collective-permute-start(f32[7,2,1,512]{3,2,1,0:T(1,128)S(1)} %get-tuple-element.66), channel_id=1, source_target_pairs={{0,4},{4,8},{8,12},{12,16},{16,20},{20,24},{24,28},{28,32},{32,36}... | collective-permute-start | bytes 86024 | tf_op jit(solution)/shard_map/ppermute | solution.py:37
  177.1 11.6 %all-to-all-start.3 = ((f32[32,14,1,2,4]{1,4,3,2,0:T(4,128)}), f32[32,14,1,2,4]{1,4,3,2,0:T(4,128)S(1)}, u32[]{:S(2)}, u32[]{:S(2)}) async-start(f32[32,14,1,2,4]{1,4,3,2,0:T(4,128)} %constant_dynamic-update-slice_fusion.120), calls=%async_computation.3 | async-start | bytes 262144 | tf_op jit(solution)/shard_map/all_to_all | solution.py:16
  191.0 3.2 %collective-permute-start.14 = (f32[7,1,18,512]{3,2,1,0:T(8,128)}, f32[7,1,18,512]{3,2,1,0:T(8,128)}, u32[]{:S(2)}, u32[]{:S(2)}) collective-permute-start(f32[7,1,18,512]{3,2,1,0:T(8,128)} %get-tuple-element.36), channel_id=1, source_target_pairs={{0,1},{1,2},{2,3},{4,5},{5,6},{6,7},{8,9},{9,10},{10,11},{12,13},{... | collective-permute-start | bytes 774152 | tf_op jit(solution)/shard_map/ppermute | solution.py:37
  200.7 4.6 %collective-permute-done.13 = f32[7,1,18,512]{3,2,1,0:T(8,128)} collective-permute-done((f32[7,1,18,512]{3,2,1,0:T(8,128)S(1)}, f32[7,1,18,512]{3,2,1,0:T(8,128)}, u32[]{:S(2)}, u32[]{:S(2)}) %collective-permute-start.13) | collective-permute-done | bytes 258080 | tf_op jit(solution)/shard_map/ppermute | solution.py:38
  208.0 2.7 copy.754
  210.7 2.9 %gather_fusion.3 = f32[256,14]{1,0:T(8,128)S(1)} fusion(f32[14,8192]{0,1:T(8,128)} %copy.754, s32[1024]{0:T(1024)S(1)} %pad_clamp_fusion), kind=kCustom, calls=%fused_computation.3.clone | custom fusion | bytes 29696 | tf_op jit(solution)/shard_map/jit(_take)/gather | solution.py:161
  216.3 3.4 %collective-permute-start.16 = (f32[7,2,1,512]{3,2,1,0:T(1,128)S(1)}, f32[7,2,1,512]{3,2,1,0:T(1,128)S(1)}, u32[]{:S(2)}, u32[]{:S(2)}) collective-permute-start(f32[7,2,1,512]{3,2,1,0:T(1,128)S(1)} %get-tuple-element.62), channel_id=1, source_target_pairs={{0,4},{4,8},{8,12},{12,16},{16,20},{20,24},{24,28},{28,32},{32,36}... | collective-permute-start | bytes 86024 | tf_op jit(solution)/shard_map/ppermute | solution.py:37
  238.7 11.6 %all-to-all-start.4 = ((f32[32,14,1,2,4]{1,4,3,2,0:T(4,128)}), f32[32,14,1,2,4]{1,4,3,2,0:T(4,128)S(1)}, u32[]{:S(2)}, u32[]{:S(2)}) async-start(f32[32,14,1,2,4]{1,4,3,2,0:T(4,128)} %constant_dynamic-update-slice_fusion.180), calls=%async_computation.4 | async-start | bytes 262144 | tf_op jit(solution)/shard_map/all_to_all | solution.py:16
  256.1 3.1 %all-to-all-done.4 = f32[32,14,1,2,4]{1,4,3,2,0:T(4,128)S(1)} async-done(((f32[32,14,1,2,4]{1,4,3,2,0:T(4,128)}), f32[32,14,1,2,4]{1,4,3,2,0:T(4,128)S(1)}, u32[]{:S(2)}, u32[]{:S(2)}) %all-to-all-start.4) | async-done | bytes 14368 | tf_op jit(solution)/shard_map/all_to_all | solution.py:16
  261.3 4.6 %collective-permute-done.18 = f32[7,1,18,512]{3,2,1,0:T(8,128)} collective-permute-done((f32[7,1,18,512]{3,2,1,0:T(8,128)S(1)}, f32[7,1,18,512]{3,2,1,0:T(8,128)}, u32[]{:S(2)}, u32[]{:S(2)}) %collective-permute-start.18) | collective-permute-done | bytes 258080 | tf_op jit(solution)/shard_map/ppermute | solution.py:38
  (398 shorter events, 145.8 us)
Async XLA Ops:
  1.8 62.0 %collective-permute-start.1 = (f32[7,2,1,512]{3,2,1,0:T(1,128)S(1)}, f32[7,2,1,512]{3,2,1,0:T(1,128)S(1)}, u32[]{:S(2)}, u32[]{:S(2)}) collective-permute-start(f32[7,2,1,512]{3,2,1,0:T(1,128)S(1)} %get-tuple-element.75), channel_id=1, source_target_pairs={{4,0},{8,4},{12,8},{16,12},{20,16},{24,20},{28,24},{32,28},{36,32}... | collective-permute-start | bytes 86024 | tf_op jit(solution)/shard_map/ppermute | solution.py:38
  6.1 57.7 %collective-permute-start = (f32[7,2,1,512]{3,2,1,0:T(1,128)S(1)}, f32[7,2,1,512]{3,2,1,0:T(1,128)S(1)}, u32[]{:S(2)}, u32[]{:S(2)}) collective-permute-start(f32[7,2,1,512]{3,2,1,0:T(1,128)S(1)} %get-tuple-element.74), channel_id=1, source_target_pairs={{0,4},{4,8},{8,12},{12,16},{16,20},{20,24},{24,28},{28,32},{32,36}... | collective-permute-start | bytes 86024 | tf_op jit(solution)/shard_map/ppermute | solution.py:37
  13.2 21.7 %all-to-all-start = ((f32[32,2,1]{1,2,0:T(1,128)}), f32[32,2,1]{1,2,0:T(1,128)S(1)}, u32[]{:S(2)}, u32[]{:S(2)}) async-start(f32[32,2,1]{1,2,0:T(1,128)} %copy.723), calls=%async_computation | async-start | bytes 32768 | tf_op jit(solution)/shard_map/all_to_all | solution.py:98
  58.7 14.2 %all-to-all-start.1 = ((f32[32,14,1,2,4]{1,4,3,2,0:T(4,128)}), f32[32,14,1,2,4]{1,4,3,2,0:T(4,128)S(1)}, u32[]{:S(2)}, u32[]{:S(2)}) async-start(f32[32,14,1,2,4]{1,4,3,2,0:T(4,128)} %constant_dynamic-update-slice_fusion), calls=%async_computation.1 | async-start | bytes 262144 | tf_op jit(solution)/shard_map/all_to_all | solution.py:16
  65.3 11.0 %collective-permute-start.3 = (f32[7,1,18,512]{3,2,1,0:T(8,128)}, f32[7,1,18,512]{3,2,1,0:T(8,128)}, u32[]{:S(2)}, u32[]{:S(2)}) collective-permute-start(f32[7,1,18,512]{3,2,1,0:T(8,128)} %get-tuple-element.40), channel_id=1, source_target_pairs={{0,1},{1,2},{2,3},{4,5},{5,6},{6,7},{8,9},{9,10},{10,11},{12,13},{... | collective-permute-start | bytes 774152 | tf_op jit(solution)/shard_map/ppermute | solution.py:37
  69.5 11.4 %collective-permute-start.2 = (f32[7,1,18,512]{3,2,1,0:T(8,128)S(1)}, f32[7,1,18,512]{3,2,1,0:T(8,128)}, u32[]{:S(2)}, u32[]{:S(2)}) collective-permute-start(f32[7,1,18,512]{3,2,1,0:T(8,128)S(1)} %get-tuple-element.41), channel_id=1, source_target_pairs={{1,0},{2,1},{3,2},{5,4},{6,5},{7,6},{9,8},{10,9},{11,10},{13,12},{... | collective-permute-start | bytes 774152 | tf_op jit(solution)/shard_map/ppermute | solution.py:38
  89.3 6.0 %collective-permute-start.10 = (f32[14,32,2,4]{0,3,2,1:T(4,128)S(1)}, f32[14,32,2,4]{0,3,2,1:T(4,128)S(1)}, u32[]{:S(2)}, u32[]{:S(2)}) collective-permute-start(f32[14,32,2,4]{0,3,2,1:T(4,128)S(1)} %bitcast.788), channel_id=1, source_target_pairs={{0,128},{128,0},{1,129},{129,1},{2,130},{130,2},{3,131},{131,3},{4... | collective-permute-start | bytes 43016 | tf_op jit(solution)/shard_map/ppermute | solution.py:27
  89.5 36.6 %collective-permute-start.7 = (f32[7,2,1,512]{3,2,1,0:T(1,128)S(1)}, f32[7,2,1,512]{3,2,1,0:T(1,128)S(1)}, u32[]{:S(2)}, u32[]{:S(2)}) collective-permute-start(f32[7,2,1,512]{3,2,1,0:T(1,128)S(1)} %get-tuple-element.71), channel_id=1, source_target_pairs={{4,0},{8,4},{12,8},{16,12},{20,16},{24,20},{28,24},{32,28},{36,32}... | collective-permute-start | bytes 86024 | tf_op jit(solution)/shard_map/ppermute | solution.py:38
  92.0 34.0 %collective-permute-start.6 = (f32[7,2,1,512]{3,2,1,0:T(1,128)S(1)}, f32[7,2,1,512]{3,2,1,0:T(1,128)S(1)}, u32[]{:S(2)}, u32[]{:S(2)}) collective-permute-start(f32[7,2,1,512]{3,2,1,0:T(1,128)S(1)} %get-tuple-element.70), channel_id=1, source_target_pairs={{0,4},{4,8},{8,12},{12,16},{16,20},{20,24},{24,28},{28,32},{32,36}... | collective-permute-start | bytes 86024 | tf_op jit(solution)/shard_map/ppermute | solution.py:37
  114.3 20.6 %all-to-all-start.2 = ((f32[32,14,1,2,4]{1,4,3,2,0:T(4,128)}), f32[32,14,1,2,4]{1,4,3,2,0:T(4,128)S(1)}, u32[]{:S(2)}, u32[]{:S(2)}) async-start(f32[32,14,1,2,4]{1,4,3,2,0:T(4,128)} %constant_dynamic-update-slice_fusion.60), calls=%async_computation.2 | async-start | bytes 262144 | tf_op jit(solution)/shard_map/all_to_all | solution.py:16
  127.6 9.9 %collective-permute-start.9 = (f32[7,1,18,512]{3,2,1,0:T(8,128)}, f32[7,1,18,512]{3,2,1,0:T(8,128)}, u32[]{:S(2)}, u32[]{:S(2)}) collective-permute-start(f32[7,1,18,512]{3,2,1,0:T(8,128)} %get-tuple-element.38), channel_id=1, source_target_pairs={{0,1},{1,2},{2,3},{4,5},{5,6},{6,7},{8,9},{9,10},{10,11},{12,13},{... | collective-permute-start | bytes 774152 | tf_op jit(solution)/shard_map/ppermute | solution.py:37
  131.1 11.3 %collective-permute-start.8 = (f32[7,1,18,512]{3,2,1,0:T(8,128)}, f32[7,1,18,512]{3,2,1,0:T(8,128)}, u32[]{:S(2)}, u32[]{:S(2)}) collective-permute-start(f32[7,1,18,512]{3,2,1,0:T(8,128)} %get-tuple-element.39), channel_id=1, source_target_pairs={{1,0},{2,1},{3,2},{5,4},{6,5},{7,6},{9,8},{10,9},{11,10},{13,12},{... | collective-permute-start | bytes 774152 | tf_op jit(solution)/shard_map/ppermute | solution.py:38
  152.1 6.0 %collective-permute-start.15 = (f32[14,32,2,4]{0,3,2,1:T(4,128)S(1)}, f32[14,32,2,4]{0,3,2,1:T(4,128)S(1)}, u32[]{:S(2)}, u32[]{:S(2)}) collective-permute-start(f32[14,32,2,4]{0,3,2,1:T(4,128)S(1)} %bitcast.789), channel_id=1, source_target_pairs={{0,128},{128,0},{1,129},{129,1},{2,130},{130,2},{3,131},{131,3},{4... | collective-permute-start | bytes 43016 | tf_op jit(solution)/shard_map/ppermute | solution.py:27
  152.2 36.5 %collective-permute-start.12 = (f32[7,2,1,512]{3,2,1,0:T(1,128)S(1)}, f32[7,2,1,512]{3,2,1,0:T(1,128)S(1)}, u32[]{:S(2)}, u32[]{:S(2)}) collective-permute-start(f32[7,2,1,512]{3,2,1,0:T(1,128)S(1)} %get-tuple-element.67), channel_id=1, source_target_pairs={{4,0},{8,4},{12,8},{16,12},{20,16},{24,20},{28,24},{32,28},{36,32}... | collective-permute-start | bytes 86024 | tf_op jit(solution)/shard_map/ppermute | solution.py:38
  154.7 34.0 %collective-permute-start.11 = (f32[7,2,1,512]{3,2,1,0:T(1,128)S(1)}, f32[7,2,1,512]{3,2,1,0:T(1,128)S(1)}, u32[]{:S(2)}, u32[]{:S(2)}) collective-permute-start(f32[7,2,1,512]{3,2,1,0:T(1,128)S(1)} %get-tuple-element.66), channel_id=1, source_target_pairs={{0,4},{4,8},{8,12},{12,16},{16,20},{20,24},{24,28},{28,32},{32,36}... | collective-permute-start | bytes 86024 | tf_op jit(solution)/shard_map/ppermute | solution.py:37
  177.1 20.5 %all-to-all-start.3 = ((f32[32,14,1,2,4]{1,4,3,2,0:T(4,128)}), f32[32,14,1,2,4]{1,4,3,2,0:T(4,128)S(1)}, u32[]{:S(2)}, u32[]{:S(2)}) async-start(f32[32,14,1,2,4]{1,4,3,2,0:T(4,128)} %constant_dynamic-update-slice_fusion.120), calls=%async_computation.3 | async-start | bytes 262144 | tf_op jit(solution)/shard_map/all_to_all | solution.py:16
  191.0 9.6 %collective-permute-start.14 = (f32[7,1,18,512]{3,2,1,0:T(8,128)}, f32[7,1,18,512]{3,2,1,0:T(8,128)}, u32[]{:S(2)}, u32[]{:S(2)}) collective-permute-start(f32[7,1,18,512]{3,2,1,0:T(8,128)} %get-tuple-element.36), channel_id=1, source_target_pairs={{0,1},{1,2},{2,3},{4,5},{5,6},{6,7},{8,9},{9,10},{10,11},{12,13},{... | collective-permute-start | bytes 774152 | tf_op jit(solution)/shard_map/ppermute | solution.py:37
  194.2 11.0 %collective-permute-start.13 = (f32[7,1,18,512]{3,2,1,0:T(8,128)S(1)}, f32[7,1,18,512]{3,2,1,0:T(8,128)}, u32[]{:S(2)}, u32[]{:S(2)}) collective-permute-start(f32[7,1,18,512]{3,2,1,0:T(8,128)S(1)} %get-tuple-element.37), channel_id=1, source_target_pairs={{1,0},{2,1},{3,2},{5,4},{6,5},{7,6},{9,8},{10,9},{11,10},{13,12},{... | collective-permute-start | bytes 774152 | tf_op jit(solution)/shard_map/ppermute | solution.py:38
  213.7 6.0 %collective-permute-start.20 = (f32[14,32,2,4]{0,3,2,1:T(4,128)S(1)}, f32[14,32,2,4]{0,3,2,1:T(4,128)S(1)}, u32[]{:S(2)}, u32[]{:S(2)}) collective-permute-start(f32[14,32,2,4]{0,3,2,1:T(4,128)S(1)} %bitcast.787), channel_id=1, source_target_pairs={{0,128},{128,0},{1,129},{129,1},{2,130},{130,2},{3,131},{131,3},{4... | collective-permute-start | bytes 43016 | tf_op jit(solution)/shard_map/ppermute | solution.py:27
  213.8 36.5 %collective-permute-start.17 = (f32[7,2,1,512]{3,2,1,0:T(1,128)S(1)}, f32[7,2,1,512]{3,2,1,0:T(1,128)S(1)}, u32[]{:S(2)}, u32[]{:S(2)}) collective-permute-start(f32[7,2,1,512]{3,2,1,0:T(1,128)S(1)} %get-tuple-element.63), channel_id=1, source_target_pairs={{4,0},{8,4},{12,8},{16,12},{20,16},{24,20},{28,24},{32,28},{36,32}... | collective-permute-start | bytes 86024 | tf_op jit(solution)/shard_map/ppermute | solution.py:38
  216.3 34.0 %collective-permute-start.16 = (f32[7,2,1,512]{3,2,1,0:T(1,128)S(1)}, f32[7,2,1,512]{3,2,1,0:T(1,128)S(1)}, u32[]{:S(2)}, u32[]{:S(2)}) collective-permute-start(f32[7,2,1,512]{3,2,1,0:T(1,128)S(1)} %get-tuple-element.62), channel_id=1, source_target_pairs={{0,4},{4,8},{8,12},{12,16},{16,20},{20,24},{24,28},{28,32},{32,36}... | collective-permute-start | bytes 86024 | tf_op jit(solution)/shard_map/ppermute | solution.py:37
  238.7 20.5 %all-to-all-start.4 = ((f32[32,14,1,2,4]{1,4,3,2,0:T(4,128)}), f32[32,14,1,2,4]{1,4,3,2,0:T(4,128)S(1)}, u32[]{:S(2)}, u32[]{:S(2)}) async-start(f32[32,14,1,2,4]{1,4,3,2,0:T(4,128)} %constant_dynamic-update-slice_fusion.180), calls=%async_computation.4 | async-start | bytes 262144 | tf_op jit(solution)/shard_map/all_to_all | solution.py:16
  252.6 8.7 %collective-permute-start.19 = (f32[7,1,18,512]{3,2,1,0:T(8,128)}, f32[7,1,18,512]{3,2,1,0:T(8,128)}, u32[]{:S(2)}, u32[]{:S(2)}) collective-permute-start(f32[7,1,18,512]{3,2,1,0:T(8,128)} %get-tuple-element.34), channel_id=1, source_target_pairs={{0,1},{1,2},{2,3},{4,5},{5,6},{6,7},{8,9},{9,10},{10,11},{12,13},{... | collective-permute-start | bytes 774152 | tf_op jit(solution)/shard_map/ppermute | solution.py:37
  254.8 11.1 %collective-permute-start.18 = (f32[7,1,18,512]{3,2,1,0:T(8,128)S(1)}, f32[7,1,18,512]{3,2,1,0:T(8,128)}, u32[]{:S(2)}, u32[]{:S(2)}) collective-permute-start(f32[7,1,18,512]{3,2,1,0:T(8,128)S(1)} %get-tuple-element.35), channel_id=1, source_target_pairs={{1,0},{2,1},{3,2},{5,4},{6,5},{7,6},{9,8},{10,9},{11,10},{13,12},{... | collective-permute-start | bytes 774152 | tf_op jit(solution)/shard_map/ppermute | solution.py:38
  (13 other events, 325.5 us)
